TPU v7x, 32 devices: a whole 2x2x4 slice. The times are simulated.
32 devices in a mesh: layer: 4 (over y, x), lat: 8 (over z, core).
Axes of the slice: x: 2, y: 2, z: 4, core: 2. Of those that a mesh axis runs over, the one named last changes fastest.
Arguments:
- activations: bfloat16 [8, 512, 2048], P(None, None, 'layer'), may hold values from -6 to 6
- targets: bfloat16 [8, 512, 2048], P(None, None, 'layer'), may hold values from -6 to 6
- encoder: bfloat16 [8, 2048, 8192], P(None, 'layer', 'lat'), may hold values from -0.125 to 0.125
- bias: float32 [8, 8192], P(None, 'lat'), may hold values from -3 to 3
- decoder: bfloat16 [36, 8192, 2048], P(None, 'lat', 'layer'), may hold values from -0.75 to 0.75
- active: int32 [8, 512, 64], replicated, may hold values from 0 to 8191, all different within a row
Outputs:
- grad_encoder: bfloat16 [8, 2048, 8192], P(None, 'layer', 'lat')
- grad_bias: float32 [8, 8192], P(None, 'lat')
- grad_decoder: bfloat16 [36, 8192, 2048], P(None, 'lat', 'layer')
Inputs may be any that keep to these rules, and one draw needn't show every extreme that they name: `active`: each row names 64 different latents.
All inputs are finite; a program needn't handle non-finite values.
Results may differ from a plain program's by a relative error of at most 0.0064.
Values may be sent and summed in bfloat16 or wider, within the bound.
A program may use at most 256 MiB of HBM per device.

v0:
```python
import jax
import jax.numpy as jnp
from jax import lax
from jax.sharding import PartitionSpec as P

LAYERS = 8


def pair_index(source, target):
    return source * LAYERS - source * (source - 1) // 2 + (target - source)


def on_device(activations, targets, encoder, bias, decoder, active):
    tokens = activations.shape[1]
    lat_width = encoder.shape[2]
    first = lax.axis_index("lat") * lat_width
    columns = first + jnp.arange(lat_width, dtype=jnp.int32)
    masks = jnp.stack(
        [
            jnp.any(active[source][:, :, None] == columns[None, None, :], axis=1)
            for source in range(LAYERS)
        ]
    ).astype(jnp.float32)
    partial_value = jnp.einsum(
        "ltd,ldf->ltf", activations, encoder, preferred_element_type=jnp.float32
    )
    preact = lax.psum(partial_value, "layer") + bias[:, None, :]
    latent_act = (preact * masks).astype(jnp.bfloat16)
    rebuilt_list = []
    for target in range(LAYERS):
        summed = jnp.dot(
            latent_act[0], decoder[pair_index(0, target)], preferred_element_type=jnp.float32
        )
        for source in range(1, target + 1):
            summed = summed + jnp.dot(
                latent_act[source],
                decoder[pair_index(source, target)],
                preferred_element_type=jnp.float32,
            )
        rebuilt_list.append(summed)
    rebuilt = jnp.stack(rebuilt_list)
    complete = lax.psum(rebuilt, "lat")
    errors = (complete - targets.astype(jnp.float32)).astype(jnp.bfloat16)
    by_tokens = (((0,), (0,)), ((), ()))
    by_width = (((1,), (1,)), ((), ()))
    grad_pairs = []
    for source in range(LAYERS):
        for target in range(source, LAYERS):
            grad_pairs.append(
                lax.dot_general(
                    latent_act[source],
                    errors[target],
                    by_tokens,
                    preferred_element_type=jnp.float32,
                ).astype(jnp.bfloat16)
            )
    grad_decoder = jnp.stack(grad_pairs)
    grad_list = []
    for source in range(LAYERS):
        summed = lax.dot_general(
            errors[source],
            decoder[pair_index(source, source)],
            by_width,
            preferred_element_type=jnp.float32,
        )
        for target in range(source + 1, LAYERS):
            summed = summed + lax.dot_general(
                errors[target],
                decoder[pair_index(source, target)],
                by_width,
                preferred_element_type=jnp.float32,
            )
        grad_list.append(summed)
    grad_partial = jnp.stack(grad_list)
    block_rows = tokens // lax.axis_size("layer")
    share_rows = lax.psum_scatter(grad_partial, "layer", scatter_dimension=1, tiled=True)
    mask_rows = lax.dynamic_slice_in_dim(masks, lax.axis_index("layer") * block_rows, block_rows, 1)
    grad_pre = lax.all_gather(
        (share_rows * mask_rows).astype(jnp.bfloat16), "layer", axis=1, tiled=True
    )
    grad_encoder = jnp.einsum(
        "ltd,ltf->ldf", activations, grad_pre, preferred_element_type=jnp.float32
    ).astype(jnp.bfloat16)
    grad_bias = jnp.sum(grad_pre.astype(jnp.float32), axis=1)
    return (grad_encoder, grad_bias, grad_decoder)


def solution(mesh):
    placed = (
        P(None, None, "layer"),
        P(None, None, "layer"),
        P(None, "layer", "lat"),
        P(None, "lat"),
        P(None, "lat", "layer"),
        P(),
    )
    return jax.shard_map(
        on_device,
        mesh=mesh,
        in_specs=placed,
        out_specs=(P(None, "layer", "lat"), P(None, "lat"), P(None, "lat", "layer")),
        check_vma=False,
    )
```

profile of v0, /device:TPU:0, one launch (start us, length us, event | category | flops | bytes accessed | tf_op | source)
XLA Modules:
  0.0 1017.3 jit_solution(10485353639587241992)
XLA Ops:
  7.2 15.4 %fusion.266 = f32[8,512,1024]{2,1,0:T(8,128)} fusion(bf16[8,512,512]{2,1,0:T(8,128)(2,1)} %param.6, bf16[8,512,1024]{2,1,0:T(8,128)(2,1)} %param.8), kind=kOutput, calls=%fused_computation.385 | convolution fusion | flops 4294967296 | bytes 29360128 | tf_op jit(solution)/shard_map/ltd,ldf->ltf/dot_general | solution.py:24
  25.0 192.2 %compare_reduce_fusion = (pred[512,1024]{1,0:T(8,128)(4,1)S(1)}, pred[512,1024]{1,0:T(8,128)(4,1)S(1)}, pred[512,1024]{1,0:T(8,128)(4,1)S(1)}, pred[512,1024]{1,...) fusion(s32[512,64]{1,0:T(8,128)S(1)} %copy.26, ...), kind=kLoop, calls=%fused_computation | loop fusion | flops 532676608 | bytes 5246976 | tf_op jit(solution)/shard_map/reduce_or | solution.py:20
  223.9 108.9 %all-reduce.3.cloned.1.call-done = f32[8,512,1024]{2,1,0:T(8,128)} async-done(((f32[8,512,1024]{2,1,0:T(8,128)}), f32[8,512,1024]{2,1,0:T(8,128)}) %all-reduce.3.cloned.1.call-update) | async-done | bytes 16777232 | tf_op jit(solution)/shard_map/psum | solution.py:27
  332.8 9.7 select_convert_fusion
  342.5 5.7 fusion.102
  409.9 13.2 %convolution_add_fusion.24 = f32[512,512]{1,0:T(8,128)} fusion(f32[512,512]{1,0:T(8,128)S(1)} %fusion.172, bf16[36,1024,512]{2,1,0:T(8,128)(2,1)S(1)} %bitcast.587, bf16[8,512,1024]{2,1,0:T(8,128)(2,1)S(1)} %select_convert_fusion), kind=kOutput, calls=%fused_computation.99 | convolution fusion | flops 537133056 | bytes 4194304 | tf_op jit(solution)/shard_map/dot_general | solution.py:35
  443.3 176.7 %all-reduce.5.cloned.1.call-done = f32[8,512,512]{2,1,0:T(8,128)} async-done(((f32[8,512,512]{2,1,0:T(8,128)}), f32[8,512,512]{2,1,0:T(8,128)}) %all-reduce.5.cloned.1.call-update) | async-done | bytes 8388624 | tf_op jit(solution)/shard_map/psum | solution.py:42
  619.9 6.0 subtract_convert_fusion
  636.6 3.3 fusion.187
  639.9 3.3 fusion.191
  643.3 3.3 fusion.119
  649.8 3.3 fusion.154
  653.1 3.3 fusion.167
  656.4 3.3 fusion.177
  659.7 3.3 fusion.184
  672.9 3.3 fusion.113
  679.5 3.3 fusion.148
  682.8 3.7 fusion.161
  692.4 3.3 fusion.107
  699.0 3.3 fusion.104
  702.3 5.1 bitcast_dynamic-update-slice_fusion.7
  707.4 7.2 bitcast_dynamic-update-slice_fusion.6
  714.7 3.7 bitcast_dynamic-update-slice_fusion.5
  719.2 3.7 bitcast_dynamic-update-slice_fusion.4
  723.0 3.5 bitcast_dynamic-update-slice_fusion.3
  726.5 3.3 bitcast_dynamic-update-slice_fusion.2
  736.6 153.8 %reduce-scatter.2.cloned.1.call-done = f32[8,128,1024]{2,1,0:T(8,128)} async-done(((f32[8,512,1024]{2,1,0:T(8,128)}), f32[8,128,1024]{2,1,0:T(8,128)}) %reduce-scatter.2.cloned.1.call-update) | async-done | bytes 4194320 | tf_op jit(solution)/shard_map/reduce_scatter | solution.py:76
  890.4 4.6 multiply_convert_fusion
  964.1 18.5 %all-gather.2.cloned.1.call-done = bf16[8,512,1024]{2,1,0:T(8,128)(2,1)} async-done(((bf16[8,128,1024]{2,1,0:T(8,128)(2,1)}), bf16[8,512,1024]{2,1,0:T(8,128)(2,1)}) %all-gather.2.cloned.1.call-update) | async-done | bytes 8388624 | tf_op jit(solution)/shard_map/all_gather | solution.py:78
  982.6 10.5 %convert_bitcast_fusion = bf16[8,512,1024]{1,2,0:T(8,128)(2,1)} fusion(bf16[8,512,1024]{2,1,0:T(8,128)(2,1)} %all-gather.2.cloned.1.call-done, bf16[8,512,512]{2,1,0:T(8,128)(2,1)} %param.6), kind=kOutput, calls=%fused_computation.10 | convolution fusion | flops 4299161600 | bytes 20971520 | tf_op jit(solution)/shard_map/ltd,ltf->ldf/dot_general | solution.py:81
  993.1 11.4 %copy.28 = bf16[8,512,1024]{2,1,0:T(8,128)(2,1)} copy(bf16[8,512,1024]{1,2,0:T(8,128)(2,1)} %convert_bitcast_fusion) | data formatting | bytes 16777216
  1004.4 5.9 convert_reduce_fusion
  (166 shorter events, 203.6 us)
Async XLA Ops:
  7.2 325.6 %all-reduce.3.cloned.1.call-start = ((), (), s32[]{:S(2)}) async-start(), calls=%async_computation.1 | async-start | bytes 33554432 | tf_op jit(solution)/shard_map/psum | solution.py:27
  22.6 1.2 copy-start.10
  22.6 597.4 %all-reduce.5.cloned.1.call-start = ((), (), s32[]{:S(2)}) async-start(), calls=%async_computation.2 | async-start | bytes 16777216 | tf_op jit(solution)/shard_map/psum | solution.py:42
  24.3 308.5 %copy-start.11 = (f32[8,1024]{1,0:T(8,128)S(1)}, f32[8,1024]{1,0:T(8,128)}, u32[]{:S(2)}) copy-start(f32[8,1024]{1,0:T(8,128)} %param.9) | copy-start | bytes 98308
  332.8 38.9 %slice-start = ((s8[37748736]{0:T(1024)(128)(4,1)}), s8[4194304]{0:T(1024)(128)(4,1)S(1)}, s32[]{:S(2)}) async-start(s8[37748736]{0:T(1024)(128)(4,1)} %bitcast.586), calls=%async_computation.5 | async-start | bytes 8388608
  332.8 38.9 %slice-start.1 = ((s8[37748736]{0:T(1024)(128)(4,1)}), s8[4194304]{0:T(1024)(128)(4,1)S(1)}, s32[]{:S(2)}) async-start(s8[37748736]{0:T(1024)(128)(4,1)} %bitcast.586), calls=%async_computation.6 | async-start | bytes 8388608
  332.8 38.9 %slice-start.2 = ((s8[37748736]{0:T(1024)(128)(4,1)}), s8[4194304]{0:T(1024)(128)(4,1)S(1)}, s32[]{:S(2)}) async-start(s8[37748736]{0:T(1024)(128)(4,1)} %bitcast.586), calls=%async_computation.7 | async-start | bytes 8388608
  332.8 38.9 %slice-start.3 = ((s8[37748736]{0:T(1024)(128)(4,1)}), s8[4194304]{0:T(1024)(128)(4,1)S(1)}, s32[]{:S(2)}) async-start(s8[37748736]{0:T(1024)(128)(4,1)} %bitcast.586), calls=%async_computation.8 | async-start | bytes 8388608
  342.5 99.0 %copy-start.9 = (bf16[8,512,1024]{2,1,0:T(8,128)(2,1)}, bf16[8,512,1024]{2,1,0:T(8,128)(2,1)S(1)}, u32[]{:S(2)}) copy-start(bf16[8,512,1024]{2,1,0:T(8,128)(2,1)S(1)} %select_convert_fusion) | copy-start | bytes 25165828
  342.5 29.2 %slice-start.4 = ((s8[37748736]{0:T(1024)(128)(4,1)}), s8[4194304]{0:T(1024)(128)(4,1)S(1)}, s32[]{:S(2)}) async-start(s8[37748736]{0:T(1024)(128)(4,1)} %bitcast.586), calls=%async_computation.9 | async-start | bytes 8388608
  350.3 21.4 %slice-start.5 = ((s8[37748736]{0:T(1024)(128)(4,1)}), s8[4194304]{0:T(1024)(128)(4,1)S(1)}, s32[]{:S(2)}) async-start(s8[37748736]{0:T(1024)(128)(4,1)} %bitcast.586), calls=%async_computation.10 | async-start | bytes 8388608
  356.4 15.4 %slice-start.6 = ((s8[37748736]{0:T(1024)(128)(4,1)}), s8[4194304]{0:T(1024)(128)(4,1)S(1)}, s32[]{:S(2)}) async-start(s8[37748736]{0:T(1024)(128)(4,1)} %bitcast.586), calls=%async_computation.11 | async-start | bytes 8388608
  360.4 11.4 %slice-start.7 = ((s8[37748736]{0:T(1024)(128)(4,1)}), s8[4194304]{0:T(1024)(128)(4,1)S(1)}, s32[]{:S(2)}) async-start(s8[37748736]{0:T(1024)(128)(4,1)} %bitcast.586), calls=%async_computation.12 | async-start | bytes 8388608
  366.4 5.4 slice-start.8
  426.0 10.5 %copy-start.13 = (f32[512,512]{1,0:T(8,128)S(1)}, f32[512,512]{1,0:T(8,128)}, u32[]{:S(2)}) copy-start(f32[512,512]{1,0:T(8,128)} %convolution_add_fusion.19) | copy-start | bytes 3145732
  427.7 10.5 %copy-start.12 = (f32[512,512]{1,0:T(8,128)S(1)}, f32[512,512]{1,0:T(8,128)}, u32[]{:S(2)}) copy-start(f32[512,512]{1,0:T(8,128)} %convolution_add_fusion.14) | copy-start | bytes 3145732
  443.2 447.2 %reduce-scatter.2.cloned.1.call-start = ((), (), s32[]{:S(2)}) async-start(), calls=%async_computation.3 | async-start | bytes 20971520 | tf_op jit(solution)/shard_map/reduce_scatter | solution.py:76
  626.0 107.1 %copy-start = (bf16[8,512,512]{2,1,0:T(8,128)(2,1)}, bf16[8,512,512]{2,1,0:T(8,128)(2,1)S(1)}, u32[]{:S(2)}) copy-start(bf16[8,512,512]{2,1,0:T(8,128)(2,1)S(1)} %subtract_convert_fusion) | copy-start | bytes 12582916
  714.7 3.7 copy-start.5
  714.7 3.7 copy-start.6
  714.7 3.7 copy-start.7
  714.7 4.5 copy-start.8
  719.2 7.2 copy-start.3
  719.2 7.2 copy-start.4
  723.0 6.8 copy-start.2
  736.4 246.2 %all-gather.2.cloned.1.call-start = ((), (), s32[]{:S(2)}) async-start(), calls=%async_computation.4 | async-start | bytes 10485760 | tf_op jit(solution)/shard_map/all_gather | solution.py:78
  895.0 6.5 copy-start.1
  898.2 12.4 %slice-start.9 = ((s8[8388608]{0:T(1024)(128)(4,1)}), s8[4194304]{0:T(1024)(128)(4,1)S(1)}, s32[]{:S(2)}) async-start(s8[8388608]{0:T(1024)(128)(4,1)} %bitcast.588), calls=%async_computation.14 | async-start | bytes 8388608
  904.5 6.1 slice-start.10
Sparse Core Ops, SparseCore 0:
  22.7 310.0 all-reduce.2
  443.3 176.5 all-reduce.4
  736.5 153.8 reduce-scatter.1
  895.1 87.4 all-gather.1
where the time goes:
time: 1030 us; the launch traced here: 1020 us
  waiting for transfers between devices  458 us (44%)
  matrix products  305 us (30%)
  other arithmetic  218 us (21%)
  local copies, waits for them, and re-layouts  21.2 us (2%)
  between operations  14.7 us (1%)
    reduce_or x1, other arithmetic, on_device(): jnp.any(active[source][:, :, None] == columns[None, None, :], axis=1)  192 us
    psum x1, waiting for transfers between devices, on_device(): complete = lax.psum(rebuilt, 'lat')  177 us
    reduce_scatter x1, waiting for transfers between devices, on_device(): lax.psum_scatter(grad_partial, 'layer', scatter_dimension=1, tiled=True)  154 us
    psum x1, waiting for transfers between devices, on_device(): preact = lax.psum(partial_value, 'layer') + bias[:, None, :]  109 us
    dot_general x28, matrix products, on_device(): lax.dot_general(errors[target], decoder[pair_index(source, target)], by_w...  85.2 us
    dot_general x28, matrix products, on_device(): jnp.dot(latent_act[source], decoder[pair_index(source, target)], preferre...  76.7 us
    dot_general x36, matrix products, on_device(): lax.dot_general(latent_act[source], errors[target], by_tokens, preferred_...  69.1 us
    dot_general x8, matrix products, on_device(): lax.dot_general(errors[source], decoder[pair_index(source, source)], by_w...  24.2 us
  transfers between devices with their start and end apart: 4, of which 4 were waited for; matrix products, arithmetic and copies ran while one was open for 26% of the time, Pallas kernels for 0%

commit v1 on v0

--- a/solution.py
+++ b/solution.py
@@ -39,7 +39,9 @@
             )
         rebuilt_list.append(summed)
     rebuilt = jnp.stack(rebuilt_list)
-    complete = lax.psum(rebuilt, "lat")
+    complete = rebuilt
+    for hop in (1, 2, 4):
+        complete = complete + lax.ppermute(complete, "lat", [(dev, dev ^ hop) for dev in range(8)])
     errors = (complete - targets.astype(jnp.float32)).astype(jnp.bfloat16)
     by_tokens = (((0,), (0,)), ((), ()))
     by_width = (((1,), (1,)), ((), ()))

time: 1030 us -> 1440 us (1.40)
  waiting for transfers between devices: 458 us -> 837 us
  other arithmetic: 218 us -> 246 us
    ppermute x0 -> x3, waiting for transfers between devices: none -> 555 us  [on_device(): lax.ppermute(complete, 'lat', [(dev, dev ^ hop) for dev in range(8)])]
    psum x1 -> x0, waiting for transfers between devices: 177 us -> none  [on_device(): complete = lax.psum(rebuilt, 'lat')]
    add x0 -> x2, other arithmetic: none -> 22.5 us  [on_device(): complete + lax.ppermute(complete, 'lat', [(dev, dev ^ hop) for dev in ran...]
  transfers between devices with their start and end apart: 4 -> 6, of which waited for: 4 -> 6; matrix products, arithmetic and copies ran while one was open for 26% -> 19% of each run, Pallas kernels for 0% -> 0%
where the time goes in v1:
time: 1440 us; the launch traced here: 1430 us
  waiting for transfers between devices  837 us (58%)
  matrix products  303 us (21%)
  other arithmetic  246 us (17%)
  local copies, waits for them, and re-layouts  24.7 us (2%)
  between operations  14.7 us (1%)
    ppermute x3, waiting for transfers between devices, on_device(): lax.ppermute(complete, 'lat', [(dev, dev ^ hop) for dev in range(8)])  555 us
    reduce_or x1, other arithmetic, on_device(): jnp.any(active[source][:, :, None] == columns[None, None, :], axis=1)  192 us
    reduce_scatter x1, waiting for transfers between devices, on_device(): lax.psum_scatter(grad_partial, 'layer', scatter_dimension=1, tiled=True)  155 us
    psum x1, waiting for transfers between devices, on_device(): preact = lax.psum(partial_value, 'layer') + bias[:, None, :]  109 us
    dot_general x28, matrix products, on_device(): lax.dot_general(errors[target], decoder[pair_index(source, target)], by_w...  83.9 us
    dot_general x28, matrix products, on_device(): jnp.dot(latent_act[source], decoder[pair_index(source, target)], preferre...  76.5 us
    dot_general x36, matrix products, on_device(): lax.dot_general(latent_act[source], errors[target], by_tokens, preferred_...  69.1 us
  transfers between devices with their start and end apart: 6, of which 6 were waited for; matrix products, arithmetic and copies ran while one was open for 19% of the time, Pallas kernels for 0%

profile of v1, /device:TPU:0, one launch (start us, length us, event | category | flops | bytes accessed | tf_op | source)
XLA Modules:
  0.0 1429.4 jit_solution(8310707014659480301)
XLA Ops:
  7.2 15.4 %fusion.266 = f32[8,512,1024]{2,1,0:T(8,128)} fusion(bf16[8,512,512]{2,1,0:T(8,128)(2,1)} %param.6, bf16[8,512,1024]{2,1,0:T(8,128)(2,1)} %param.8), kind=kOutput, calls=%fused_computation.385 | convolution fusion | flops 4294967296 | bytes 29360128 | tf_op jit(solution)/shard_map/ltd,ldf->ltf/dot_general | solution.py:24
  25.0 192.2 %compare_reduce_fusion = (pred[512,1024]{1,0:T(8,128)(4,1)S(1)}, pred[512,1024]{1,0:T(8,128)(4,1)S(1)}, pred[512,1024]{1,0:T(8,128)(4,1)S(1)}, pred[512,1024]{1,...) fusion(s32[512,64]{1,0:T(8,128)S(1)} %copy.26, ...), kind=kLoop, calls=%fused_computation | loop fusion | flops 532676608 | bytes 5246976 | tf_op jit(solution)/shard_map/reduce_or | solution.py:20
  223.9 108.9 %all-reduce.2.cloned.1.call-done = f32[8,512,1024]{2,1,0:T(8,128)} async-done(((f32[8,512,1024]{2,1,0:T(8,128)}), f32[8,512,1024]{2,1,0:T(8,128)}) %all-reduce.2.cloned.1.call-update) | async-done | bytes 16777232 | tf_op jit(solution)/shard_map/psum | solution.py:27
  332.8 9.6 select_convert_fusion
  342.5 5.7 fusion.103
  366.0 3.4 convolution_add_fusion.6
  442.7 3.4 copy-done.2
  446.1 13.3 collective-permute-done
  459.4 11.3 add.234
  472.1 181.3 %collective-permute-done.1 = f32[8,512,512]{2,1,0:T(8,128)} collective-permute-done((f32[8,512,512]{2,1,0:T(8,128)}, f32[8,512,512]{2,1,0:T(8,128)}, u32[]{:S(2)}, u32[]{:S(2)}) %collective-permute-start.1) | collective-permute-done | bytes 8388640 | tf_op jit(solution)/shard_map/ppermute | solution.py:44
  653.4 11.3 add.235
  667.1 360.2 %collective-permute-done.2 = f32[8,512,512]{2,1,0:T(8,128)} collective-permute-done((f32[8,512,512]{2,1,0:T(8,128)}, f32[8,512,512]{2,1,0:T(8,128)}, u32[]{:S(2)}, u32[]{:S(2)}) %collective-permute-start.2) | collective-permute-done | bytes 8388640 | tf_op jit(solution)/shard_map/ppermute | solution.py:44
  1027.3 11.5 subtract_convert_fusion
  1064.9 3.3 fusion.167
  1068.2 3.3 fusion.177
  1071.6 3.3 fusion.184
  1084.8 3.3 fusion.113
  1088.1 3.4 fusion.132
  1104.0 3.4 fusion.107
  1110.7 3.4 fusion.89
  1114.1 4.5 bitcast_dynamic-update-slice_fusion.7
  1118.6 7.3 bitcast_dynamic-update-slice_fusion.6
  1125.9 3.6 bitcast_dynamic-update-slice_fusion.5
  1130.4 3.6 bitcast_dynamic-update-slice_fusion.4
  1134.1 3.5 bitcast_dynamic-update-slice_fusion.3
  1140.9 3.3 bitcast_dynamic-update-slice_fusion.1
  1147.6 154.8 %reduce-scatter.2.cloned.1.call-done = f32[8,128,1024]{2,1,0:T(8,128)} async-done(((f32[8,512,1024]{2,1,0:T(8,128)}), f32[8,128,1024]{2,1,0:T(8,128)}) %reduce-scatter.2.cloned.1.call-update) | async-done | bytes 4194320 | tf_op jit(solution)/shard_map/reduce_scatter | solution.py:78
  1302.4 4.6 multiply_convert_fusion
  1376.1 18.5 %all-gather.2.cloned.1.call-done = bf16[8,512,1024]{2,1,0:T(8,128)(2,1)} async-done(((bf16[8,128,1024]{2,1,0:T(8,128)(2,1)}), bf16[8,512,1024]{2,1,0:T(8,128)(2,1)}) %all-gather.2.cloned.1.call-update) | async-done | bytes 8388624 | tf_op jit(solution)/shard_map/all_gather | solution.py:80
  1394.6 10.5 convert_bitcast_fusion
  1405.1 11.4 copy.28
  1416.5 5.9 convert_reduce_fusion
  (173 shorter events, 232.3 us)
Async XLA Ops:
  7.2 325.6 %all-reduce.2.cloned.1.call-start = ((), (), s32[]{:S(2)}) async-start(), calls=%async_computation.1 | async-start | bytes 33554432 | tf_op jit(solution)/shard_map/psum | solution.py:27
  22.6 1.2 copy-start.11
  22.6 1279.8 %reduce-scatter.2.cloned.1.call-start = ((), (), s32[]{:S(2)}) async-start(), calls=%async_computation.2 | async-start | bytes 20971520 | tf_op jit(solution)/shard_map/reduce_scatter | solution.py:78
  24.3 308.5 %copy-start.12 = (f32[8,1024]{1,0:T(8,128)S(1)}, f32[8,1024]{1,0:T(8,128)}, u32[]{:S(2)}) copy-start(f32[8,1024]{1,0:T(8,128)} %param.9) | copy-start | bytes 98308
  332.8 39.1 %slice-start = ((s8[37748736]{0:T(1024)(128)(4,1)}), s8[4194304]{0:T(1024)(128)(4,1)S(1)}, s32[]{:S(2)}) async-start(s8[37748736]{0:T(1024)(128)(4,1)} %bitcast.586), calls=%async_computation.4 | async-start | bytes 8388608
  332.8 39.1 %slice-start.1 = ((s8[37748736]{0:T(1024)(128)(4,1)}), s8[4194304]{0:T(1024)(128)(4,1)S(1)}, s32[]{:S(2)}) async-start(s8[37748736]{0:T(1024)(128)(4,1)} %bitcast.586), calls=%async_computation.5 | async-start | bytes 8388608
  332.8 39.1 %slice-start.2 = ((s8[37748736]{0:T(1024)(128)(4,1)}), s8[4194304]{0:T(1024)(128)(4,1)S(1)}, s32[]{:S(2)}) async-start(s8[37748736]{0:T(1024)(128)(4,1)} %bitcast.586), calls=%async_computation.6 | async-start | bytes 8388608
  332.8 39.1 %slice-start.3 = ((s8[37748736]{0:T(1024)(128)(4,1)}), s8[4194304]{0:T(1024)(128)(4,1)S(1)}, s32[]{:S(2)}) async-start(s8[37748736]{0:T(1024)(128)(4,1)} %bitcast.586), calls=%async_computation.7 | async-start | bytes 8388608
  342.4 16.0 %copy-start.10 = (bf16[8,512,1024]{2,1,0:T(8,128)(2,1)}, bf16[8,512,1024]{2,1,0:T(8,128)(2,1)S(1)}, u32[]{:S(2)}) copy-start(bf16[8,512,1024]{2,1,0:T(8,128)(2,1)S(1)} %select_convert_fusion) | copy-start | bytes 25165828
  342.4 29.5 %slice-start.4 = ((s8[37748736]{0:T(1024)(128)(4,1)}), s8[4194304]{0:T(1024)(128)(4,1)S(1)}, s32[]{:S(2)}) async-start(s8[37748736]{0:T(1024)(128)(4,1)} %bitcast.586), calls=%async_computation.8 | async-start | bytes 8388608
  350.3 21.7 %slice-start.5 = ((s8[37748736]{0:T(1024)(128)(4,1)}), s8[4194304]{0:T(1024)(128)(4,1)S(1)}, s32[]{:S(2)}) async-start(s8[37748736]{0:T(1024)(128)(4,1)} %bitcast.586), calls=%async_computation.9 | async-start | bytes 8388608
  356.3 15.7 %slice-start.6 = ((s8[37748736]{0:T(1024)(128)(4,1)}), s8[4194304]{0:T(1024)(128)(4,1)S(1)}, s32[]{:S(2)}) async-start(s8[37748736]{0:T(1024)(128)(4,1)} %bitcast.586), calls=%async_computation.10 | async-start | bytes 8388608
  360.3 11.7 slice-start.7
  366.0 6.0 slice-start.8
  425.0 9.9 copy-start.14
  428.0 8.8 copy-start.13
  442.7 3.4 copy-start.2
  446.1 13.3 collective-permute-start
  470.6 182.8 %collective-permute-start.1 = (f32[8,512,512]{2,1,0:T(8,128)}, f32[8,512,512]{2,1,0:T(8,128)}, u32[]{:S(2)}, u32[]{:S(2)}) collective-permute-start(f32[8,512,512]{2,1,0:T(8,128)} %add.234), channel_id=1, source_target_pairs={{0,2},{1,3},{2,0},{3,1},{4,6},{5,7},{6,4},{7,5},{8,10},{9,11},{10,... | collective-permute-start | bytes 25165832 | tf_op jit(solution)/shard_map/ppermute | solution.py:44
  664.7 362.6 %collective-permute-start.2 = (f32[8,512,512]{2,1,0:T(8,128)}, f32[8,512,512]{2,1,0:T(8,128)}, u32[]{:S(2)}, u32[]{:S(2)}) collective-permute-start(f32[8,512,512]{2,1,0:T(8,128)} %add.235), channel_id=1, source_target_pairs={{0,4},{1,5},{2,6},{3,7},{4,0},{5,1},{6,2},{7,3},{8,12},{9,13},{10,... | collective-permute-start | bytes 25165832 | tf_op jit(solution)/shard_map/ppermute | solution.py:44
  1038.8 7.0 copy-start
  1125.9 3.7 copy-start.6
  1125.9 3.7 copy-start.7
  1125.9 3.7 copy-start.8
  1125.9 4.5 copy-start.9
  1130.4 7.1 copy-start.4
  1130.4 7.1 copy-start.5
  1134.1 6.8 copy-start.3
  1147.5 247.1 %all-gather.2.cloned.1.call-start = ((), (), s32[]{:S(2)}) async-start(), calls=%async_computation.3 | async-start | bytes 10485760 | tf_op jit(solution)/shard_map/all_gather | solution.py:80
  1307.0 6.5 copy-start.1
  1310.2 12.4 slice-start.9
  1316.6 6.1 slice-start.10
Sparse Core Ops, SparseCore 0:
  22.7 310.0 all-reduce.1
  1147.6 154.7 reduce-scatter.1
  1307.1 87.4 all-gather.1
